TPU v7x, 32 devices: a whole 2x2x4 slice. The times are simulated.
32 devices in a mesh: row: 4 (over y, x), col: 8 (over z, core).
Axes of the slice: x: 2, y: 2, z: 4, core: 2. Of those that a mesh axis runs over, the one named last changes fastest.
Arguments:
- panel_one: bfloat16 [16384, 2048], P(('row', 'col')), may hold values from -0.796875 to 0.796875
- panel_two: bfloat16 [16384, 2048], P(('row', 'col')), may hold values from -6 to 6
- inverse_one: bfloat16 [2048, 2048], P(None, 'col'), as said below
- inverse_two: bfloat16 [2048, 2048], P(None, 'col'), as said below
- update_list: int32 [32, 2], P(('row', 'col')), may hold values from -1 to 1, as said below
Outputs:
- factor_one: bfloat16 [16384, 2048], P(('row', 'col'))
- factor_two: bfloat16 [16384, 2048], P(('row', 'col'))
Inputs may be any that keep to these rules, and one draw needn't show every extreme that they name: `inverse_one`: upper triangular: zero below the diagonal, diagonal entries between 0.5 and 1.5. `inverse_two`: upper triangular: zero below the diagonal, diagonal entries between 0.5 and 1.5. `update_list`: entry (d, j) names a block among the 2 first-supernode blocks of device d, or is -1 (no update). The named blocks of one device are distinct, a device's live entries come before its -1 entries, and every entry of devices 0 to 3 is live.
All inputs are finite; a program needn't handle non-finite values.
Results may differ from a plain program's by a relative error of at most 0.0056.
Values may be sent and summed in bfloat16 or wider, within the bound.
A program may use at most 128 MiB of HBM per device.

v0:
```python
import jax
import jax.numpy as jnp
from jax import lax
from jax.sharding import PartitionSpec as P

SN = 2048
B = 256
OWNERS = 4


def broadcast(value, axis, source):
    kept = jnp.where(lax.axis_index(axis) == source, value, 0).astype(value.dtype)
    return lax.psum(kept, axis)


def apply_rows(left, piece):
    return jnp.dot(left, piece, preferred_element_type=jnp.float32)


def body(panel_one, panel_two, inverse_one, inverse_two, update_list):
    factor_one = apply_rows(
        panel_one, lax.all_gather(inverse_one, "col", axis=1, tiled=True)
    ).astype(jnp.bfloat16)
    blocks = factor_one.reshape(-1, B, SN)
    entries = update_list[0]
    chosen = blocks[jnp.maximum(entries, 0)]
    selected = jnp.where(
        (entries >= 0)[:, None, None], chosen, jnp.zeros((), jnp.bfloat16)
    ).reshape(-1, SN)
    pieces = []
    for owner in range(OWNERS):
        pieces.append(broadcast(selected, ("row", "col"), owner))
    column_panel = jnp.concatenate(pieces, axis=0)
    update = lax.dot_general(
        selected, column_panel, (((1,), (1,)), ((), ())), preferred_element_type=jnp.float32
    )
    modified = (panel_two.astype(jnp.float32) - update).astype(jnp.bfloat16)
    factor_two = apply_rows(modified, lax.all_gather(inverse_two, "col", axis=1, tiled=True))
    return (factor_one, factor_two.astype(jnp.bfloat16))


def solution(mesh):
    return jax.shard_map(
        body,
        mesh=mesh,
        in_specs=(
            P(("row", "col"), None),
            P(("row", "col"), None),
            P(None, "col"),
            P(None, "col"),
            P(("row", "col"), None),
        ),
        out_specs=(P(("row", "col"), None), P(("row", "col"), None)),
        check_vma=False,
    )
```

profile of v0, /device:TPU:0, one launch (start us, length us, event | category | flops | bytes accessed | tf_op | source)
XLA Modules:
  0.0 385.2 jit_solution(17785649631808427820)
XLA Ops:
  7.2 0.0 copy-start
  7.2 0.0 copy-start.2
  7.2 0.0 all-gather.3.cloned.1.call-start
  7.2 0.7 all-gather.3.cloned.1.call-update
  7.9 0.0 all-gather.5.cloned.1.call-start
  8.0 0.7 all-gather.5.cloned.1.call-update
  8.7 0.0 all-reduce.3.cloned.1.call-start
  8.7 0.0 copy-done.2
  8.7 0.1 broadcast_in_dim.23
  8.9 86.0 %all-gather.3.cloned.1.call-done = bf16[2048,2048]{1,0:T(8,128)(2,1)} async-done(((bf16[2048,256]{1,0:T(8,128)(2,1)}), bf16[2048,2048]{1,0:T(8,128)(2,1)}) %all-gather.3.cloned.1.call-update) | async-done | bytes 8388624 | tf_op jit(solution)/shard_map/all_gather | solution.py:22
  94.8 0.0 copy-done
  94.8 9.0 %convolution_convert_fusion.1 = bf16[512,2048]{1,0:T(8,128)(2,1)} fusion(bf16[512,2048]{1,0:T(8,128)(2,1)S(1)} %copy-done, bf16[2048,2048]{1,0:T(8,128)(2,1)} %all-gather.3.cloned.1.call-done), kind=kOutput, calls=%fused_computation.11 | convolution fusion | flops 4296015872 | bytes 12582912 | tf_op jit(solution)/shard_map/dot_general | solution.py:17
  103.8 3.7 gather_fusion
  107.5 3.3 broadcast_select_fusion.3
  110.8 0.0 copy-start.1
  110.8 2.9 broadcast_select_fusion.2
  113.7 0.4 copy-done.1
  114.1 0.0 all-reduce.3.cloned.1.call-update
  114.1 63.0 %all-gather.5.cloned.1.call-done = bf16[2048,2048]{1,0:T(8,128)(2,1)} async-done(((bf16[2048,256]{1,0:T(8,128)(2,1)}), bf16[2048,2048]{1,0:T(8,128)(2,1)}) %all-gather.5.cloned.1.call-update) | async-done | bytes 8388624 | tf_op jit(solution)/shard_map/all_gather | solution.py:38
  177.1 183.9 %all-reduce.3.cloned.1.call-done = (bf16[512,2048]{1,0:T(8,128)(2,1)}, bf16[512,2048]{1,0:T(8,128)(2,1)}, bf16[512,2048]{1,0:T(8,128)(2,1)}, bf16[512,2048]{1,0:T(8,128)(2,1)}) async-done(((bf16[512,2048]{1,0:T(8,128)(2,1)}, bf16[512,2048]{1,0:T(8,128)(2,1)}, bf16[512,2048]{1,0:T(8,128)(2,1)}, bf16[512,2048]{1,0:T(8,128)(2,1)}), (bf16[512,2048]{1,0:T(8,128)(2,1)}, bf16[512,2048]{1,0:T(8,128)(2,1)}, ...) | async-done | bytes 8388624 | tf_op jit(solution)/shard_map/psum | solution.py:13
  361.0 17.7 %convolution_convert_fusion = bf16[512,2048]{1,0:T(8,128)(2,1)} fusion(bf16[2048,2048]{1,0:T(8,128)(2,1)} %all-gather.5.cloned.1.call-done, bf16[512,2048]{1,0:T(8,128)(2,1)} %param.6, bf16[512,2048]{1,0:T(8,128)(2,1)} %copy-done.1, bf16[512,2048]{1,0:T(8,128)(2,1)} %get-tuple-element.2, bf16[512,2048]{1,0:T(8,128)(2,1)} %get-tuple-element.3, ...), kind=kOutput, calls=%fused_computation.10 | convolution fusion | flops 8627683328 | bytes 23068672 | tf_op jit(solution)/shard_map/dot_general | solution.py:17
  (4 shorter events, 0.0 us)
Async XLA Ops:
  7.2 87.7 %copy-start = (bf16[512,2048]{1,0:T(8,128)(2,1)S(1)}, bf16[512,2048]{1,0:T(8,128)(2,1)}, u32[]{:S(2)}) copy-start(bf16[512,2048]{1,0:T(8,128)(2,1)} %param.5) | copy-start | bytes 6291460
  7.2 1.5 copy-start.2
  7.2 87.6 %all-gather.3.cloned.1.call-start = ((), (), s32[]{:S(2)}) async-start(), calls=%async_computation | async-start | bytes 9437184 | tf_op jit(solution)/shard_map/all_gather | solution.py:22
  7.9 169.2 %all-gather.5.cloned.1.call-start = ((), (), s32[]{:S(2)}) async-start(), calls=%async_computation.1 | async-start | bytes 9437184 | tf_op jit(solution)/shard_map/all_gather | solution.py:38
  8.7 352.3 %all-reduce.3.cloned.1.call-start = ((), (), s32[]{:S(2)}) async-start(), calls=%async_computation.2 | async-start | bytes 16777216 | tf_op jit(solution)/shard_map/psum | solution.py:13
  110.8 3.3 copy-start.1
Sparse Core Ops, SparseCore 0:
  9.6 85.1 all-gather.2
  96.4 80.6 all-gather.4
  183.7 177.2 all-reduce.2
where the time goes:
time: 385 us
  waiting for transfers between devices  334 us (87%)
  matrix products  26.7 us (7%)
  between operations  13.8 us (4%)
  other arithmetic  6.21 us (2%)
  local copies, waits for them, and re-layouts  4.16 us (1%)
    psum x1, waiting for transfers between devices, broadcast(): return lax.psum(kept, axis)  184 us
    all_gather x1, waiting for transfers between devices, body(): lax.all_gather(inverse_one, 'col', axis=1, tiled=True)  86 us
    all_gather x1, waiting for transfers between devices, body(): lax.all_gather(inverse_two, 'col', axis=1, tiled=True)  63 us
    dot_general x2, matrix products, apply_rows(): return jnp.dot(left, piece, preferred_element_type=jnp.float32)  26.7 us
  transfers between devices with their start and end apart: 3, of which 3 were waited for; matrix products, arithmetic and copies ran while one was open for 5% of the time, Pallas kernels for 0%

commit v1 on v0

v1 whole, which is shorter than its diff:
```python
import functools

import jax
import jax.numpy as jnp
from jax import lax
from jax.experimental import pallas as pl
from jax.experimental.pallas import tpu as pltpu
from jax.sharding import PartitionSpec as P

MESH = pl.DeviceIdType.MESH
CORES = 2


def kernel(R, C, entries, p1, psel, p2, i1, i2, f1, f2, g1, g2, pg, cp, sel, mod, send, recv, local):
    Z = C // CORES
    T = R // 2
    rows, SN = p1.shape
    W = i1.shape[1]
    sources = pg.shape[0]
    order = [p ^ (p >> 1) for p in range(R)]
    row, col = lax.axis_index("row"), lax.axis_index("col")
    z, k = col // CORES, col % CORES
    pos, right, left = jnp.int32(0), jnp.int32(0), jnp.int32(0)
    for p in range(R):
        here = row == order[p]
        pos = jnp.where(here, p, pos)
        right = jnp.where(here, order[(p + 1) % R], right)
        left = jnp.where(here, order[(p + R - 1) % R], left)
    sibling = (row, z * CORES + 1 - k)

    items = [("i", zs, i1, g1, (zs + 1) * CORES * W) for zs in range(Z)]
    items += [("p", zs, psel, pg, rows) for zs in range(sources // CORES)]
    items += [("i", zs, i2, g2, (zs + 1) * CORES * W) for zs in range(Z)]
    pending = []

    def remote(src, dst, ssem, rsem, to):
        return pltpu.make_async_remote_copy(
            src_ref=src, dst_ref=dst, send_sem=ssem, recv_sem=rsem, device_id=to, device_id_type=MESH
        )

    def begin(when, make):
        def go():
            make().start()

        if when is None:
            go()
        else:
            pl.when(when)(go)
        pending.append((when, make))

    def arrive(when, dst, rsem):
        def go():
            remote(dst, dst, send.at[0, 0], rsem, sibling).wait_recv()

        if when is None:
            go()
        else:
            pl.when(when)(go)

    def piece(n, p, step, side):
        kind, zs, own, buf, H = items[n]
        h = H // R
        start, size = p * h, h
        if step == T:
            if h % 32 == 0:
                size = h // 2
                start = start + side * size
            elif side == 1:
                return None
        return buf.at[zs * CORES + k, pl.ds(pl.multiple_of(start, 8), size)]

    def active(n):
        return None if items[n][0] == "p" else z != items[n][1]

    def along_z(n, src):
        kind, zs, own, buf, H = items[n]
        for zd in range(Z):
            if zd != zs:
                begin(
                    z == zs,
                    lambda zd=zd: remote(
                        src, piece(n, pos, 0, 0), send.at[n, zd], recv.at[n, 0], (row, zd * CORES + k)
                    ),
                )

    def ring(n, step):
        base = Z + 2 * (step - 1)
        one = piece(n, lax.rem(pos + R - (step - 1), R), step, 0)
        two = piece(n, lax.rem(pos + step - 1, R), step, 1)
        for side, ref, to in ((0, one, right), (1, two, left)):
            if ref is not None:
                begin(
                    active(n),
                    lambda side=side, ref=ref, to=to: remote(
                        ref, ref, send.at[n, base + side], recv.at[n, 2 * step - 1 + side], (to, col)
                    ),
                )

    def ring_wait(n, step):
        one = piece(n, lax.rem(pos + R - step, R), step, 0)
        two = piece(n, lax.rem(pos + step, R), step, 1)
        for side, ref in ((0, one), (1, two)):
            if ref is not None:
                arrive(active(n), ref, recv.at[n, 2 * step - 1 + side])

    last_send, last_recv = Z + 2 * T, 2 * T + 1

    def whole(n, core):
        kind, zs, own, buf, H = items[n]
        return buf.at[zs * CORES + core, pl.ds(0, H)]

    def first(n):
        kind, zs, own, buf, H = items[n]
        if kind == "i":
            @pl.when(z == zs)
            def _():
                pltpu.make_async_copy(own.at[pl.ds(0, H)], whole(n, k), local.at[n]).start()

            h = H // R
            along_z(n, own.at[pl.ds(pl.multiple_of(pos * h, 8), h)])
            begin(
                z == zs,
                lambda: remote(
                    own.at[pl.ds(0, H)], whole(n, k), send.at[n, last_send], recv.at[n, last_recv], sibling
                ),
            )
        else:
            h = H // R
            origin = (z == zs) & (row == 0)

            @pl.when(origin)
            def _():
                pltpu.make_async_copy(
                    own.at[pl.ds(0, h)], buf.at[zs * CORES + k, pl.ds(0, h)], local.at[n]
                ).start()

            for p in range(1, R):
                begin(
                    origin,
                    lambda p=p: remote(
                        own.at[pl.ds(p * h, h)],
                        buf.at[zs * CORES + k, pl.ds(p * h, h)],
                        send.at[n, last_send + p],
                        recv.at[n, 0],
                        (order[p], col),
                    ),
                )

    def stage_a(n):
        kind, zs, own, buf, H = items[n]
        if kind == "i":
            arrive(z != zs, piece(n, pos, 0, 0), recv.at[n, 0])
        else:
            h = H // R
            origin = (z == zs) & (row == 0)

            @pl.when(origin)
            def _():
                pltpu.make_async_copy(
                    own.at[pl.ds(0, h)], buf.at[zs * CORES + k, pl.ds(0, h)], local.at[n]
                ).wait()

            arrive(jnp.logical_not(origin), piece(n, pos, 0, 0), recv.at[n, 0])
            along_z(n, piece(n, pos, 0, 0))
        ring(n, 1)

    def stage_b(n):
        for step in range(1, T):
            ring_wait(n, step)
            ring(n, step + 1)

    def stage_c(n):
        ring_wait(n, T)
        begin(
            active(n),
            lambda: remote(
                whole(n, k), whole(n, k), send.at[n, last_send], recv.at[n, last_recv], sibling
            ),
        )

    def stage_d(n):
        kind, zs, own, buf, H = items[n]
        arrive(None, whole(n, 1 - k), recv.at[n, last_recv])
        if kind == "i":
            @pl.when(z == zs)
            def _():
                pltpu.make_async_copy(own.at[pl.ds(0, H)], whole(n, k), local.at[n]).wait()

    def columns(out, left_of, buf, zs):
        for c in range(zs * CORES, (zs + 1) * CORES):
            depth = (c + 1) * W
            out[:, c * W:(c + 1) * W] = jnp.dot(
                left_of(depth), buf[c, 0:depth, :], preferred_element_type=jnp.float32
            ).astype(out.dtype)

    B = rows // entries.shape[1]

    def choose():
        for j in range(entries.shape[1]):
            entry = entries[0, j]
            value = jnp.zeros((B, SN), jnp.bfloat16)
            for b in range(entries.shape[1]):
                value = jnp.where(entry == b, f1[b * B:(b + 1) * B, :], value)
            sel[j * B:(j + 1) * B, :] = value

    def update(zs):
        for s in range(zs * CORES, (zs + 1) * CORES):
            for zz in range(Z):
                columns(cp, lambda depth: pg[s, :, 0:depth], g1, zz)
            span = rows // 2
            for half in range(2):
                product = lax.dot_general(
                    sel[...],
                    cp[half * span:(half + 1) * span, :],
                    (((1,), (1,)), ((), ())),
                    preferred_element_type=jnp.float32,
                )
                place = slice(s * rows + half * span, s * rows + (half + 1) * span)
                mod[:, place] = (p2[:, place].astype(jnp.float32) - product).astype(jnp.bfloat16)

    def compute(n):
        kind, zs, own, buf, H = items[n]
        if kind == "p":
            update(zs)
        elif n < Z:
            columns(f1, lambda depth: p1[:, 0:depth], g1, zs)
            if n == Z - 1:
                choose()
        else:
            columns(f2, lambda depth: mod[:, 0:depth], g2, zs)

    barrier = pltpu.get_barrier_semaphore()
    for d in range(1, R):
        pl.semaphore_signal(barrier, inc=1, device_id=(lax.rem(row + d, R), col), device_id_type=MESH)
    for d in range(1, Z):
        pl.semaphore_signal(
            barrier, inc=1, device_id=(row, lax.rem(z + d, Z) * CORES + k), device_id_type=MESH
        )
    pl.semaphore_signal(barrier, inc=1, device_id=sibling, device_id_type=MESH)
    pl.semaphore_wait(barrier, R - 1 + Z - 1 + 1)

    N = len(items)
    for n in range(N):
        if items[n][0] == "p":
            first(n)
    for n in range(N):
        if items[n][0] == "i":
            first(n)
    for t in range(N + 3):
        if t < N:
            stage_a(t)
        if 0 <= t - 1 < N:
            stage_b(t - 1)
        if 0 <= t - 2 < N:
            stage_c(t - 2)
        if 0 <= t - 3 < N:
            stage_d(t - 3)
            compute(t - 3)
    for when, make in pending:
        if when is None:
            make().wait_send()
        else:
            pl.when(when)(lambda make=make: make().wait_send())


def body(R, C, panel_one, panel_two, inverse_one, inverse_two, update_list):
    rows, SN = panel_one.shape
    W = inverse_one.shape[1]
    count = update_list.shape[1]
    B = rows // count
    entries = update_list[0]
    blocks = panel_one.reshape(count, B, SN)
    chosen = jnp.zeros((count, B, SN), jnp.bfloat16)
    for b in range(count):
        chosen = jnp.where((entries == b)[:, None, None], blocks[b][None], chosen)
    chosen = chosen.reshape(rows, SN)
    sources = SN // rows
    items = 2 * (C // CORES) + sources // CORES
    vmem = pl.BlockSpec(memory_space=pltpu.VMEM)
    return pl.pallas_call(
        functools.partial(kernel, R, C),
        out_shape=[jax.ShapeDtypeStruct((rows, SN), jnp.bfloat16)] * 2,
        in_specs=[pl.BlockSpec(memory_space=pltpu.SMEM)] + [vmem] * 5,
        out_specs=[vmem, vmem],
        scratch_shapes=[
            pltpu.VMEM((C, SN, W), jnp.bfloat16),
            pltpu.VMEM((C, SN, W), jnp.bfloat16),
            pltpu.VMEM((sources, rows, SN), jnp.bfloat16),
            pltpu.VMEM((rows, SN), jnp.bfloat16),
            pltpu.VMEM((rows, SN), jnp.bfloat16),
            pltpu.VMEM((rows, SN), jnp.bfloat16),
            pltpu.SemaphoreType.DMA((items, C // CORES + 2 * (R // 2) + R)),
            pltpu.SemaphoreType.DMA((items, 2 * (R // 2) + 2)),
            pltpu.SemaphoreType.DMA((items,)),
        ],
        compiler_params=pltpu.CompilerParams(
            collective_id=0, has_side_effects=True, vmem_limit_bytes=62 * 1024 * 1024
        ),
        name="panel",
    )(update_list, panel_one, chosen, panel_two, inverse_one, inverse_two)


def solution(mesh):
    R, C = mesh.shape["row"], mesh.shape["col"]
    return jax.shard_map(
        functools.partial(body, R, C),
        mesh=mesh,
        in_specs=(
            P(("row", "col"), None),
            P(("row", "col"), None),
            P(None, "col"),
            P(None, "col"),
            P(("row", "col"), None),
        ),
        out_specs=(P(("row", "col"), None), P(("row", "col"), None)),
        check_vma=False,
    )
```

time: 385 us -> 159 us (0.41)
  the two profiles are of different devices: /device:TPU:0 before, /device:TPU:25 now
where the time goes in v1:
time: 159 us
  Pallas kernels  150 us (94%)
  local copies, waits for them, and re-layouts  6.49 us (4%)
  other arithmetic  2.37 us (1%)
    pallas_call x1, Pallas kernels, body(): pl.pallas_call(functools.partial(kernel, R, C), out_shape=[jax.ShapeDtype...  150 us
    unnamed x4, local copies, waits for them, and re-layouts  4.63 us

profile of v1, /device:TPU:25, one launch (start us, length us, event | category | flops | bytes accessed | tf_op | source)
XLA Modules:
  0.0 159.0 jit_solution(13109536380413341938)
XLA Ops:
  0.6 0.7 compare_bitcast_fusion.1
  1.3 0.1 broadcast_in_dim.43
  1.4 0.1 broadcast_in_dim.48
  1.5 1.7 %fusion.1 = (bf16[256,2048]{1,0:T(8,128)(2,1)S(1)}, bf16[256,2048]{1,0:T(8,128)(2,1)S(1)}) fusion(bf16[512,2048]{1,0:T(8,128)(2,1)} %p1.1), kind=kLoop, calls=%fused_computation.4 | loop fusion | bytes 4194304 | tf_op jit(solution)/shard_map/slice | solution.py:275
  3.2 1.7 %fusion.psel = bf16[512,2048]{1,0:T(8,128)(2,1)} fusion(pred[512]{0:T(512)(128)(4,1)S(1)} %broadcast_in_dim.49, pred[512]{0:T(512)(128)(4,1)S(1)} %broadcast_in_dim.44, bf16[256,2048]{1,0:T(8,128)(2,1)S(1)} %get-tuple-element.3, bf16[256,2048]{1,0:T(8,128)(2,1)S(1)} %get-tuple-element.2), kind=kLoop, calls=%fused_computation.1 | loop fusion | flops 2097152 | bytes 4195328 | tf_op jit(solution)/shard_map/jit(_where)/select_n | solution.py:275
  4.9 149.5 %panel.1 = (bf16[512,2048]{1,0:T(8,128)(2,1)}, bf16[512,2048]{1,0:T(8,128)(2,1)}) custom-call(s32[1,2]{1,0:T(1,128)} %entries.1, bf16[512,2048]{1,0:T(8,128)(2,1)} %p1.1, bf16[512,2048]{1,0:T(8,128)(2,1)} %fusion.psel, bf16[512,2048]{1,0:T(8,128)(2,1)} %p2.1, bf16[2048,256]{1,0:T(8,128)(2,1)} %i1.1, bf16[2048,256]{1,0:T(8,128)(2,1)} %i2.1), custom_call_target="tpu_custom_call" | custom-call | tf_op jit(solution)/shard_map/panel/pallas_call | solution.py:280
  154.4 0.0 copy-start
  154.4 3.3 %copy.9 = bf16[512,2048]{1,0:T(8,128)(2,1)} copy(bf16[512,2048]{1,0:T(8,128)(2,1)} %get-tuple-element.8) | data formatting | bytes 4194304
  157.7 0.0 copy-done
  157.7 1.3 copy.10
  (2 shorter events, 0.0 us)
Async XLA Ops:
  154.4 3.3 %copy-start = (bf16[512,2048]{1,0:T(8,128)(2,1)S(1)}, bf16[512,2048]{1,0:T(8,128)(2,1)}, u32[]{:S(2)}) copy-start(bf16[512,2048]{1,0:T(8,128)(2,1)} %get-tuple-element.9) | copy-start | bytes 6291460

commit v2 on v1

v2 whole, which is shorter than its diff:
```python
import functools

import jax
import jax.numpy as jnp
from jax import lax
from jax.experimental import pallas as pl
from jax.experimental.pallas import tpu as pltpu
from jax.sharding import PartitionSpec as P

MESH = pl.DeviceIdType.MESH
CORES = 2
SUBS = 4


def kernel(
    R, C, entries, h1, psel, h2, i1, i2, out1, out2, p1, p2, f1, f2, g1, g2, pg, cp, sel, mod, send, recv, local, moves
):
    Z = C // CORES
    T = R // 2
    rows, SN = p1.shape
    W = i1.shape[1]
    sources = pg.shape[0]
    order = [p ^ (p >> 1) for p in range(R)]
    row, col = lax.axis_index("row"), lax.axis_index("col")
    z, k = col // CORES, col % CORES
    pos, right, left = jnp.int32(0), jnp.int32(0), jnp.int32(0)
    for p in range(R):
        here = row == order[p]
        pos = jnp.where(here, p, pos)
        right = jnp.where(here, order[(p + 1) % R], right)
        left = jnp.where(here, order[(p + R - 1) % R], left)
    sibling = (row, z * CORES + 1 - k)

    items = [("i", zs, i1, g1, 0, (zs + 1) * CORES * W) for zs in range(Z)]
    planes = sources // CORES
    span = rows // SUBS
    items += [("p", zs, psel, pg, b * span, span) for b in range(SUBS) for zs in range(planes)]
    items += [("i", zs, i2, g2, 0, (zs + 1) * CORES * W) for zs in range(Z)]
    pending = []

    def remote(src, dst, ssem, rsem, to):
        return pltpu.make_async_remote_copy(
            src_ref=src, dst_ref=dst, send_sem=ssem, recv_sem=rsem, device_id=to, device_id_type=MESH
        )

    def begin(when, make):
        def go():
            make().start()

        if when is None:
            go()
        else:
            pl.when(when)(go)
        pending.append((when, make))

    def arrive(when, dst, rsem):
        def go():
            remote(dst, dst, send.at[0, 0], rsem, sibling).wait_recv()

        if when is None:
            go()
        else:
            pl.when(when)(go)

    def piece(n, p, step, side):
        kind, zs, own, buf, base, H = items[n]
        h = H // R
        start, size = base + p * h, h
        if step == T:
            if h % 32 == 0:
                size = h // 2
                start = start + side * size
            elif side == 1:
                return None
        return buf.at[zs * CORES + k, pl.ds(pl.multiple_of(start, 8), size)]

    def active(n):
        return z != items[n][1]

    def along_z(n, src, when):
        zs = items[n][1]
        if zs > 0:
            begin(
                when,
                lambda: remote(src, piece(n, pos, 0, 0), send.at[n, 0], recv.at[n, 0], (row, col - CORES)),
            )
        if zs < Z - 1:
            begin(
                when,
                lambda: remote(src, piece(n, pos, 0, 0), send.at[n, 1], recv.at[n, 0], (row, col + CORES)),
            )

    def onward(n):
        zs = items[n][1]
        ref = piece(n, pos, 0, 0)
        if zs > 1:
            begin(
                (z < zs) & (z > 0),
                lambda: remote(ref, ref, send.at[n, 0], recv.at[n, 0], (row, col - CORES)),
            )
        if zs < Z - 2:
            begin(
                (z > zs) & (z < Z - 1),
                lambda: remote(ref, ref, send.at[n, 1], recv.at[n, 0], (row, col + CORES)),
            )

    def ring(n, step):
        base = 2 + 2 * (step - 1)
        one = piece(n, lax.rem(pos + R - (step - 1), R), step, 0)
        two = piece(n, lax.rem(pos + step - 1, R), step, 1)
        for side, ref, to in ((0, one, right), (1, two, left)):
            if ref is not None:
                begin(
                    active(n),
                    lambda side=side, ref=ref, to=to: remote(
                        ref, ref, send.at[n, base + side], recv.at[n, 2 * step - 1 + side], (to, col)
                    ),
                )

    def ring_wait(n, step):
        one = piece(n, lax.rem(pos + R - step, R), step, 0)
        two = piece(n, lax.rem(pos + step, R), step, 1)
        for side, ref in ((0, one), (1, two)):
            if ref is not None:
                arrive(active(n), ref, recv.at[n, 2 * step - 1 + side])

    last_send, last_recv = 2 + 2 * T, 2 * T + 1

    def whole(n, core):
        kind, zs, own, buf, base, H = items[n]
        return buf.at[zs * CORES + core, pl.ds(base, H)]

    def load_own(n):
        kind, zs, own, buf, base, H = items[n]
        return pltpu.make_async_copy(own.at[pl.ds(base, H)], whole(n, k), local.at[n])

    def first(n):
        kind, zs, own, buf, base, H = items[n]
        h = H // R
        if kind == "i":
            along_z(n, own.at[pl.ds(pl.multiple_of(pos * h, 8), h)], z == zs)
            begin(
                z == zs,
                lambda: remote(
                    own.at[pl.ds(0, H)], whole(n, k), send.at[n, last_send], recv.at[n, last_recv], sibling
                ),
            )
            pl.when(z == zs)(lambda: load_own(n).start())
        else:
            origin = (z == zs) & (pos == 0)
            for side, to in ((0, right), (1, left)):
                begin(
                    origin,
                    lambda side=side, to=to: remote(
                        own.at[pl.ds(base + side * (H // 2), H // 2)],
                        half(n, side),
                        send.at[n, 2 + side],
                        recv.at[n, 1 + side],
                        (to, col),
                    ),
                )
            along_z(n, own.at[pl.ds(base, h)], origin)
            begin(
                origin,
                lambda: remote(
                    own.at[pl.ds(base, H)], whole(n, k), send.at[n, last_send], recv.at[n, last_recv], sibling
                ),
            )
            pl.when(origin)(lambda: load_own(n).start())

    def half(n, side):
        kind, zs, own, buf, base, H = items[n]
        return buf.at[zs * CORES + k, pl.ds(base + side * (H // 2), H // 2)]

    def hop(n, h):
        zs = items[n][1]
        for side, at, to in ((0, h, right), (1, R - h, left)):
            when = (z == zs) & (pos == at)
            arrive(when, half(n, side), recv.at[n, 1 + side])
            if h < R - 1:
                begin(
                    when,
                    lambda side=side, to=to: remote(
                        half(n, side), half(n, side), send.at[n, 2 + side], recv.at[n, 1 + side], (to, col)
                    ),
                )
        if h == T:
            along_z(n, piece(n, pos, 0, 0), (z == zs) & (pos == h))
        elif h < T:
            along_z(n, piece(n, pos, 0, 0), (z == zs) & ((pos == h) | (pos == R - h)))
        if h == R - 1:
            begin(
                (z == zs) & (pos != 0),
                lambda: remote(
                    whole(n, k), whole(n, k), send.at[n, last_send], recv.at[n, last_recv], sibling
                ),
            )

    def stage_a(n):
        arrive(active(n), piece(n, pos, 0, 0), recv.at[n, 0])
        onward(n)
        ring(n, 1)

    def stage_b(n):
        for step in range(1, T):
            ring_wait(n, step)
            ring(n, step + 1)

    def stage_c(n):
        ring_wait(n, T)
        begin(
            active(n),
            lambda: remote(
                whole(n, k), whole(n, k), send.at[n, last_send], recv.at[n, last_recv], sibling
            ),
        )

    def stage_d(n):
        kind, zs, own, buf, base, H = items[n]
        arrive(None, whole(n, 1 - k), recv.at[n, last_recv])
        pl.when((z == zs) if kind == "i" else (z == zs) & (pos == 0))(lambda: load_own(n).wait())

    def columns(out, left_of, buf, zs):
        for c in range(zs * CORES, (zs + 1) * CORES):
            depth = (c + 1) * W
            out[:, c * W:(c + 1) * W] = jnp.dot(
                left_of(depth), buf[c, 0:depth, :], preferred_element_type=jnp.float32
            ).astype(out.dtype)

    B = rows // entries.shape[1]

    def choose():
        for j in range(entries.shape[1]):
            entry = entries[0, j]
            value = jnp.zeros((B, SN), jnp.bfloat16)
            for b in range(entries.shape[1]):
                value = jnp.where(entry == b, f1[b * B:(b + 1) * B, :], value)
            sel[j * B:(j + 1) * B, :] = value

    def update(s):
        for zz in range(Z):
            columns(cp, lambda depth: pg[s, :, 0:depth], g1, zz)
        width = rows // 2
        for part in range(2):
            product = lax.dot_general(
                sel[...],
                cp[part * width:(part + 1) * width, :],
                (((1,), (1,)), ((), ())),
                preferred_element_type=jnp.float32,
            )
            place = slice(s * rows + part * width, s * rows + (part + 1) * width)
            mod[:, place] = (p2[:, place].astype(jnp.float32) - product).astype(jnp.bfloat16)

    def factor_one(n):
        if n == 0:
            loads[0].wait()
        columns(f1, lambda depth: p1[:, 0:depth], g1, items[n][1])
        if n == Z - 1:
            stores[0].start()
            choose()
            loads[1].wait()

    def store_two(zs):
        place = pl.ds(zs * CORES * W, CORES * W)
        return pltpu.make_async_copy(f2.at[:, place], out2.at[:, place], moves.at[3 + zs])

    def factor_two(n):
        zs = items[n][1]
        columns(f2, lambda depth: mod[:, 0:depth], g2, zs)
        store_two(zs).start()

    loads = [pltpu.make_async_copy(h1, p1, moves.at[0]), pltpu.make_async_copy(h2, p2, moves.at[1])]
    stores = [pltpu.make_async_copy(f1, out1, moves.at[2])]

    barrier = pltpu.get_barrier_semaphore()
    for d in range(1, R):
        pl.semaphore_signal(barrier, inc=1, device_id=(lax.rem(row + d, R), col), device_id_type=MESH)
    for d in range(1, Z):
        pl.semaphore_signal(
            barrier, inc=1, device_id=(row, lax.rem(z + d, Z) * CORES + k), device_id_type=MESH
        )
    pl.semaphore_signal(barrier, inc=1, device_id=sibling, device_id_type=MESH)
    pl.semaphore_wait(barrier, R - 1 + Z - 1 + 1)

    N = len(items)
    P0, Q0 = Z, Z + SUBS * planes
    for n in list(range(P0, Q0)) + list(range(P0)):
        first(n)
    for load in loads:
        load.start()
    events = []
    for i in range(Z):
        events.append((0.5, first, Q0 + i))
        for stage, extra in ((stage_a, 0), (stage_b, 4), (stage_c, 7), (stage_d, 9), (factor_one, 9.1)):
            events.append((1 + i * (i + 5) / 3 + extra, stage, i))
    for b in range(SUBS):
        for zs in range(planes):
            n = P0 + b * planes + zs
            for h in range(1, R):
                events.append((4 * b + 4 * h, functools.partial(hop, h=h), n))
            for stage, extra in ((stage_a, 12), (stage_b, 16), (stage_c, 20), (stage_d, 24)):
                events.append((4 * b + extra, stage, n))
    for s in range(sources):
        events.append((4 * SUBS + 21 + s, update, s))
    for i in range(Z):
        n = Q0 + i
        for stage, key in ((stage_a, 11 + i * (i + 5) * 2 / 3), (stage_b, 15 + i * (i + 6) * 2 / 3), (stage_c, 18 + i * (i + 6) * 2 / 3)):
            events.append((key, stage, n))
        for stage, key in ((stage_d, 60 + i), (factor_two, 60.1 + i)):
            events.append((key, stage, n))
    for _, stage, n in sorted(events, key=lambda event: event[0]):
        stage(n)
    stores[0].wait()
    for zs in range(Z):
        store_two(zs).wait()
    for when, make in pending:
        if when is None:
            make().wait_send()
        else:
            pl.when(when)(lambda make=make: make().wait_send())


def body(R, C, panel_one, panel_two, inverse_one, inverse_two, update_list):
    rows, SN = panel_one.shape
    W = inverse_one.shape[1]
    count = update_list.shape[1]
    B = rows // count
    entries = update_list[0]
    blocks = panel_one.reshape(count, B, SN)
    chosen = jnp.zeros((count, B, SN), jnp.bfloat16)
    for b in range(count):
        chosen = jnp.where((entries == b)[:, None, None], blocks[b][None], chosen)
    chosen = chosen.reshape(rows, SN)
    sources = SN // rows
    items = 2 * (C // CORES) + SUBS * (sources // CORES)
    hbm = pl.BlockSpec(memory_space=pl.ANY)
    return pl.pallas_call(
        functools.partial(kernel, R, C),
        out_shape=[jax.ShapeDtypeStruct((rows, SN), jnp.bfloat16)] * 2,
        in_specs=[pl.BlockSpec(memory_space=pltpu.SMEM)] + [hbm] * 5,
        out_specs=[hbm, hbm],
        scratch_shapes=[pltpu.VMEM((rows, SN), jnp.bfloat16) for _ in range(4)]
        + [
            pltpu.VMEM((C, SN, W), jnp.bfloat16),
            pltpu.VMEM((C, SN, W), jnp.bfloat16),
            pltpu.VMEM((sources, rows, SN), jnp.bfloat16),
            pltpu.VMEM((rows, SN), jnp.bfloat16),
            pltpu.VMEM((rows, SN), jnp.bfloat16),
            pltpu.VMEM((rows, SN), jnp.bfloat16),
            pltpu.SemaphoreType.DMA((items, 3 + 2 * (R // 2))),
            pltpu.SemaphoreType.DMA((items, 2 * (R // 2) + 2)),
            pltpu.SemaphoreType.DMA((items,)),
            pltpu.SemaphoreType.DMA((3 + C // CORES,)),
        ],
        compiler_params=pltpu.CompilerParams(
            collective_id=0, has_side_effects=True, vmem_limit_bytes=62 * 1024 * 1024
        ),
        name="panel",
    )(update_list, panel_one, chosen, panel_two, inverse_one, inverse_two)


def solution(mesh):
    R, C = mesh.shape["row"], mesh.shape["col"]
    return jax.shard_map(
        functools.partial(body, R, C),
        mesh=mesh,
        in_specs=(
            P(("row", "col"), None),
            P(("row", "col"), None),
            P(None, "col"),
            P(None, "col"),
            P(("row", "col"), None),
        ),
        out_specs=(P(("row", "col"), None), P(("row", "col"), None)),
        check_vma=False,
    )
```

time: 159 us -> 143 us (0.90)
  the two profiles are of different devices: /device:TPU:25 before, /device:TPU:0 now
where the time goes in v2:
time: 143 us
  Pallas kernels  133 us (93%)
  local copies, waits for them, and re-layouts  6.49 us (5%)
  other arithmetic  2.37 us (2%)
    pallas_call x1, Pallas kernels, body(): pl.pallas_call(functools.partial(kernel, R, C), out_shape=[jax.ShapeDtype...  133 us
    unnamed x4, local copies, waits for them, and re-layouts  4.63 us

profile of v2, /device:TPU:0, one launch (start us, length us, event | category | flops | bytes accessed | tf_op | source)
XLA Modules:
  0.0 142.7 jit_solution(3889424643134608318)
XLA Ops:
  0.6 0.7 compare_bitcast_fusion.1
  1.3 0.1 broadcast_in_dim.43
  1.4 0.1 broadcast_in_dim.48
  1.5 1.7 %fusion.1 = (bf16[256,2048]{1,0:T(8,128)(2,1)S(1)}, bf16[256,2048]{1,0:T(8,128)(2,1)S(1)}) fusion(bf16[512,2048]{1,0:T(8,128)(2,1)} %h1.1), kind=kLoop, calls=%fused_computation.4 | loop fusion | bytes 4194304 | tf_op jit(solution)/shard_map/slice | solution.py:332
  3.2 1.7 %fusion.psel = bf16[512,2048]{1,0:T(8,128)(2,1)} fusion(pred[512]{0:T(512)(128)(4,1)S(1)} %broadcast_in_dim.49, pred[512]{0:T(512)(128)(4,1)S(1)} %broadcast_in_dim.44, bf16[256,2048]{1,0:T(8,128)(2,1)S(1)} %get-tuple-element.3, bf16[256,2048]{1,0:T(8,128)(2,1)S(1)} %get-tuple-element.2), kind=kLoop, calls=%fused_computation.1 | loop fusion | flops 2097152 | bytes 4195328 | tf_op jit(solution)/shard_map/jit(_where)/select_n | solution.py:332
  4.9 133.2 %panel.1 = (bf16[512,2048]{1,0:T(8,128)(2,1)}, bf16[512,2048]{1,0:T(8,128)(2,1)}) custom-call(s32[1,2]{1,0:T(1,128)} %entries.1, bf16[512,2048]{1,0:T(8,128)(2,1)} %h1.1, bf16[512,2048]{1,0:T(8,128)(2,1)} %fusion.psel, bf16[512,2048]{1,0:T(8,128)(2,1)} %h2.1, bf16[2048,256]{1,0:T(8,128)(2,1)} %i1.1, bf16[2048,256]{1,0:T(8,128)(2,1)} %i2.1), custom_call_target="tpu_custom_call" | custom-call | tf_op jit(solution)/shard_map/panel/pallas_call | solution.py:337
  138.0 0.0 copy-start
  138.0 3.3 %copy.9 = bf16[512,2048]{1,0:T(8,128)(2,1)} copy(bf16[512,2048]{1,0:T(8,128)(2,1)} %get-tuple-element.8) | data formatting | bytes 4194304
  141.4 0.0 copy-done
  141.4 1.3 copy.10
  (2 shorter events, 0.0 us)
Async XLA Ops:
  138.0 3.3 %copy-start = (bf16[512,2048]{1,0:T(8,128)(2,1)S(1)}, bf16[512,2048]{1,0:T(8,128)(2,1)}, u32[]{:S(2)}) copy-start(bf16[512,2048]{1,0:T(8,128)(2,1)} %get-tuple-element.9) | copy-start | bytes 6291460
